TPU v7x, 256 devices: a whole 4x4x8 slice. The times are simulated.
256 devices in a mesh: det: 64 (over z, y, core), tm: 4 (over x).
Axes of the slice: x: 4, y: 4, z: 8, core: 2. Of those that a mesh axis runs over, the one named last changes fastest.
Arguments:
- time_streams: float32 [64, 1, 4096], P('det', None, 'tm'), may hold values from -12 to 12
- pol_angle: float32 [64, 1, 4096], P('det', None, 'tm'), may hold values from -3.140625 to 3.140625
- offsets: int32 [64, 1, 4096], P('det', None, 'tm'), may hold values from 0 to 255
- block_slots: int32 [64, 1, 16], P('det', None, 'tm'), may hold values from 0 to 127
- hit_ids: int32 [64, 128], P('det'), may hold values from 0 to 1023, as said below
- valid_counts: int32 [64, 1], P('det'), may hold values from 1024 to 4096
- filter_taps: float32 [64, 1, 65], P('det'), may hold values from -0.75 to 0.75
- white_weight: float32 [64, 1], P('det'), may hold values from 0.5 to 2
Outputs:
- solution_map: float32 [1024, 3, 256], P('det')
- precond_residual: float32 [1024, 3, 256], P('det')
Inputs may be any that keep to these rules, and one draw needn't show every extreme that they name: `hit_ids`: slot o * 2 + c of a section names a block of o * 16 .. (o + 1) * 16 - 1, and the 2 blocks of one o in one section differ.
All inputs are finite; a program needn't handle non-finite values.
Results may differ from a plain program's by a relative error of at most 0.0003.
Values sent between devices are 32-bit elements; how exact they have to be, the bound alone decides.
A program may use at most 128 MiB of HBM per device.

v0:
```python
import jax
import jax.numpy as jnp
from jax import lax
from jax.sharding import PartitionSpec as P

BLK = 256
WIN = 256
BAND = 64
ITERS = 2
NDET = 1
TCH = 1024
BPD = 16
CAP = 2
highest = lax.Precision.HIGHEST


def with_halo(cells, sides, width):
    for axis, dim in sides:
        count = lax.axis_size(axis)
        ends = count - 1
        head = lax.slice_in_dim(cells, 0, width, axis=dim)
        tail = lax.slice_in_dim(cells, cells.shape[dim] - width, cells.shape[dim], axis=dim)
        cells = jnp.concatenate(
            [
                lax.ppermute(tail, axis, [(i, (i + 1) % count) for i in range(ends)]),
                cells,
                lax.ppermute(head, axis, [((i + 1) % count, i) for i in range(ends)]),
            ],
            axis=dim,
        )
    return cells


def lag_table(filter_taps, white_weight):
    columns = []
    for shift_lag in range(BAND + 1):
        columns.append(
            jnp.sum(
                filter_taps[..., : BAND + 1 - shift_lag] * filter_taps[..., shift_lag:], axis=-1
            )
        )
    lags = jnp.stack(columns, axis=-1)
    return lags.at[..., 0].add(white_weight)


def toeplitz_matrix(lags):
    row_index = jnp.arange(WIN + 2 * BAND, dtype=jnp.int32)[:, None]
    col_index = jnp.arange(WIN, dtype=jnp.int32)[None, :]
    distance = jnp.abs(row_index - BAND - col_index)
    inside = distance <= BAND
    clipped = jnp.minimum(distance, BAND)
    return jnp.where(inside[None], lags[:, clipped], 0.0)


def precondition(weights, residual):
    entry_aa = 1.0 + weights[:, 0]
    entry_ab = weights[:, 1]
    entry_ac = weights[:, 2]
    entry_bb = 1.0 + weights[:, 3]
    entry_bc = weights[:, 4]
    entry_cc = 1.0 + weights[:, 5]
    minor_aa = entry_bb * entry_cc - entry_bc * entry_bc
    minor_ab = entry_ac * entry_bc - entry_ab * entry_cc
    minor_ac = entry_ab * entry_bc - entry_ac * entry_bb
    minor_bb = entry_aa * entry_cc - entry_ac * entry_ac
    minor_bc = entry_ab * entry_ac - entry_aa * entry_bc
    minor_cc = entry_aa * entry_bb - entry_ab * entry_ab
    determinant = entry_aa * minor_aa + entry_ab * minor_ab + entry_ac * minor_ac
    stokes_i = residual[:, 0]
    stokes_q = residual[:, 1]
    stokes_u = residual[:, 2]
    return jnp.stack(
        [
            (minor_aa * stokes_i + minor_ab * stokes_q + minor_ac * stokes_u) / determinant,
            (minor_ab * stokes_i + minor_bb * stokes_q + minor_bc * stokes_u) / determinant,
            (minor_ac * stokes_i + minor_bc * stokes_q + minor_cc * stokes_u) / determinant,
        ],
        axis=1,
    )


def global_dot(left, right):
    return lax.psum(jnp.sum(left * right), "det")


def per_device(
    time_streams, pol_angle, offsets, block_slots, hit_ids, valid_counts, filter_taps, white_weight
):
    det_count = lax.axis_size("det")
    block_count = TCH // WIN
    lags = lag_table(filter_taps[0], white_weight[0])
    matrix = toeplitz_matrix(lags)
    hit_row = hit_ids[0]
    hit_total = hit_row.shape[0]
    span_start = lax.axis_index("tm") * TCH
    sample_time = span_start + jnp.arange(TCH, dtype=jnp.int32)
    live_mask = (
        (sample_time[None, :] < valid_counts[0][:, None])
        .astype(jnp.float32)
        .reshape(NDET, block_count, WIN)
    )
    cosine = jnp.cos(2.0 * pol_angle[0]).reshape(NDET, block_count, WIN)
    sine_term = jnp.sin(2.0 * pol_angle[0]).reshape(NDET, block_count, WIN)
    pixel_pick = (
        offsets[0].reshape(NDET, block_count, WIN, 1) == jnp.arange(BLK, dtype=jnp.int32)
    ).astype(jnp.float32)
    slot_pick = (jnp.arange(hit_total, dtype=jnp.int32)[:, None] == block_slots[0]).astype(
        jnp.float32
    )
    place_pick = (
        (hit_row.reshape(det_count, CAP) % BPD)[:, :, None] == jnp.arange(BPD, dtype=jnp.int32)
    ).astype(jnp.float32)

    def noise_filter(signal):
        padded = with_halo(signal.reshape(NDET, TCH), (("tm", 1),), BAND)
        extended = jnp.pad(padded, ((0, 0), (0, WIN - 2 * BAND)))
        leading = extended[:, :TCH].reshape(NDET, block_count, WIN)
        trailing = extended[:, WIN : WIN + TCH].reshape(NDET, block_count, WIN)[:, :, : 2 * BAND]
        window = jnp.concatenate([leading, trailing], axis=2)
        return jnp.einsum("djo,dok->djk", window, matrix, precision=highest)

    def bin_samples(components):
        comp_count = components.shape[2]
        per_block = jnp.einsum("djwp,djkw->djkp", pixel_pick, components, precision=highest)
        summed = jnp.dot(
            slot_pick, per_block.reshape(NDET * block_count, comp_count * BLK), precision=highest
        )
        return summed.reshape(hit_total, comp_count, BLK)

    def to_owner_blocks(binned):
        comp_count = binned.shape[1]
        pixel_part = binned.shape[2]
        grouped = binned.reshape(det_count, CAP, comp_count * pixel_part)
        whole_map = jnp.einsum("ocb,ocx->obx", place_pick, grouped, precision=highest)
        whole_map = whole_map.reshape(det_count * BPD, comp_count, pixel_part)
        owned_map = lax.psum_scatter(whole_map, "det", scatter_dimension=0, tiled=True)
        owned_map = lax.psum(owned_map, "tm")
        return owned_map

    filtered = noise_filter(time_streams[0].reshape(NDET, block_count, WIN) * live_mask) * live_mask
    weight = lags[:, 0][:, None, None] * live_mask
    components = jnp.stack(
        [
            filtered,
            filtered * cosine,
            filtered * sine_term,
            weight,
            weight * cosine,
            weight * sine_term,
            weight * cosine * cosine,
            weight * cosine * sine_term,
            weight * sine_term * sine_term,
        ],
        axis=2,
    )
    initial = to_owner_blocks(bin_samples(components))
    right_side = initial[:, :3]
    weights = initial[:, 3:]
    solution = jnp.zeros_like(right_side)
    residual = right_side
    descent = precondition(weights, residual)
    direction = descent
    product_now = global_dot(residual, descent)
    for iteration in range(ITERS):
        from_whole_map = lax.all_gather(direction, "det", axis=0, tiled=True)
        from_grouped = from_whole_map.reshape(det_count, BPD, 3 * BLK)
        picked = jnp.einsum("ocb,obx->ocx", place_pick, from_grouped, precision=highest)
        fetched = picked.reshape(hit_total, 3, BLK)
        apply_per_block = jnp.dot(
            slot_pick.T, fetched.reshape(hit_total, 3 * BLK), precision=highest
        )
        apply_per_block = apply_per_block.reshape(NDET, block_count, 3, BLK)
        values = jnp.einsum("djwp,djcp->djcw", pixel_pick, apply_per_block, precision=highest)
        apply_signal = (
            values[:, :, 0] + values[:, :, 1] * cosine + values[:, :, 2] * sine_term
        ) * live_mask
        apply_filtered = noise_filter(apply_signal) * live_mask
        apply_components = jnp.stack(
            [apply_filtered, apply_filtered * cosine, apply_filtered * sine_term], axis=2
        )
        image_map = to_owner_blocks(bin_samples(apply_components))
        step_size = product_now / global_dot(direction, image_map)
        solution = solution + step_size * direction
        residual = residual - step_size * image_map
        descent = precondition(weights, residual)
        if iteration + 1 < ITERS:
            product_next = global_dot(residual, descent)
            direction = descent + product_next / product_now * direction
            product_now = product_next
    return (solution, descent)


def solution(mesh):
    in_specs = (
        P("det", None, "tm"),
        P("det", None, "tm"),
        P("det", None, "tm"),
        P("det", None, "tm"),
        P("det", None),
        P("det", None),
        P("det", None, None),
        P("det", None),
    )
    out_specs = (P("det", None, None), P("det", None, None))
    return jax.shard_map(
        per_device, mesh=mesh, in_specs=in_specs, out_specs=out_specs, check_vma=False
    )
```

profile of v0, /device:TPU:1, one launch (start us, length us, event | category | flops | bytes accessed | tf_op | source)
XLA Modules:
  0.0 1986.2 jit_solution(1493701683084729770)
XLA Ops:
  8.6 3.9 collective-permute-start
  15.2 1.5 multiply_reduce_fusion.62
  20.9 1.5 multiply_reduce_fusion.58
  23.8 1.5 multiply_reduce_fusion.56
  25.3 1.5 multiply_reduce_fusion.55
  28.1 1.5 multiply_reduce_fusion.53
  32.5 1.4 multiply_reduce_fusion.50
  33.9 1.5 multiply_reduce_fusion.49
  38.2 1.5 multiply_reduce_fusion.46
  39.6 1.5 multiply_reduce_fusion.45
  44.0 1.4 multiply_reduce_fusion.42
  45.4 1.5 multiply_reduce_fusion.41
  48.3 1.5 multiply_reduce_fusion.39
  51.2 1.5 multiply_reduce_fusion.37
  52.6 1.5 multiply_reduce_fusion.36
  55.6 1.4 multiply_reduce_fusion.34
  57.0 1.5 multiply_reduce_fusion.33
  59.9 1.5 multiply_reduce_fusion.31
  64.2 1.5 multiply_reduce_fusion.28
  65.7 1.5 multiply_reduce_fusion.27
  69.9 1.5 multiply_reduce_fusion.24
  74.3 1.4 multiply_reduce_fusion.21
  77.1 1.5 multiply_reduce_fusion.19
  80.0 1.5 multiply_reduce_fusion.17
  84.2 1.5 multiply_reduce_fusion.14
  88.5 1.5 multiply_reduce_fusion.12
  91.4 1.5 multiply_reduce_fusion.10
  94.3 1.5 multiply_reduce_fusion.8
  95.8 1.5 multiply_reduce_fusion.7
  98.7 1.5 multiply_reduce_fusion.5
  101.5 1.5 multiply_reduce_fusion.65
  113.4 583.8 %gather_fusion = f32[98304]{0:T(1024)S(1)} fusion(f32[65]{0:T(128)S(1)} %bitcast_dynamic-update-slice_fusion, s32[98304]{0:T(1024)S(1)} %broadcast_clamp_fusion), kind=kCustom, calls=%fused_computation | custom fusion | bytes 1179648 | tf_op jit(solution)/shard_map/gather | solution.py:52
  701.8 7.9 fusion
  709.7 12.7 reshape.851
  722.4 14.9 copy.43
  737.3 156.0 %reduce-scatter.2.cloned.1.call-done = f32[16,9,256]{2,0,1:T(8,128)} async-done(((f32[1024,9,256]{2,0,1:T(8,128)}), f32[16,9,256]{2,0,1:T(8,128)}) %reduce-scatter.2.cloned.1.call-update) | async-done | bytes 147472 | tf_op jit(solution)/shard_map/reduce_scatter | solution.py:136
  893.6 49.2 %all-reduce.10.cloned.1.call-done = f32[16,9,256]{2,0,1:T(8,128)} async-done(((f32[16,9,256]{2,0,1:T(8,128)}), f32[16,9,256]{2,0,1:T(8,128)}) %all-reduce.10.cloned.1.call-update) | async-done | bytes 147472 | tf_op jit(solution)/shard_map/psum | solution.py:137
  942.8 1.5 add_divide_fusion.8
  944.2 1.5 add_divide_fusion.7
  948.4 80.5 %all-gather.3.cloned.1.call-done = f32[1024,3,256]{2,0,1:T(8,128)} async-done(((f32[16,3,256]{2,0,1:T(8,128)}), f32[1024,3,256]{2,0,1:T(8,128)}) %all-gather.3.cloned.1.call-update) | async-done | bytes 3145744 | tf_op jit(solution)/shard_map/all_gather | solution.py:165
  1028.9 6.0 copy.44
  1034.9 4.8 reshape.852
  1039.7 2.0 fusion.33
  1045.4 3.1 collective-permute-start.2
  1049.9 2.9 collective-permute-done.3
  1053.0 1.4 convolution_select_fusion.1
  1056.8 2.9 fusion.16
  1059.7 3.3 reshape.858
  1064.9 191.2 %all-reduce.12.cloned.1.call-done = f32[1024,3,256]{2,1,0:T(4,128)} async-done(((f32[1024,3,256]{2,1,0:T(4,128)}), f32[1024,3,256]{2,1,0:T(4,128)}) %all-reduce.12.cloned.1.call-update) | async-done | bytes 3145744
  1257.0 13.5 psum.51
  1271.2 130.2 %all-reduce.5 = (f32[]{:T(128)}, f32[]{:T(128)}) all-reduce(f32[]{:T(128)} %get-tuple-element.19, f32[]{:T(128)} %get-tuple-element.18), channel_id=1, replica_groups=mesh['det'=64,'tm'=4] {'det'}, use_global_device_ids=true, to_apply=%region_68.69 | all-reduce | flops 2 | bytes 16 | tf_op jit(solution)/shard_map/psum | solution.py:83
  1404.0 124.6 %psum.53 = f32[]{:T(128)} all-reduce(f32[]{:T(128)} %multiply_reduce_fusion.1), channel_id=1, replica_groups=mesh['det'=64,'tm'=4] {'det'}, use_global_device_ids=true, to_apply=%region_74.75 | all-reduce | flops 1 | bytes 8 | tf_op jit(solution)/shard_map/psum | solution.py:83
  1530.8 73.7 %all-gather.5.cloned.1.call-done = f32[1024,3,256]{2,0,1:T(8,128)} async-done(((f32[16,3,256]{2,0,1:T(8,128)}), f32[1024,3,256]{2,0,1:T(8,128)}) %all-gather.5.cloned.1.call-update) | async-done | bytes 3145744 | tf_op jit(solution)/shard_map/all_gather | solution.py:165
  1604.5 6.0 copy.50
  1610.5 4.8 reshape.859
  1615.3 2.0 fusion.32
  1621.0 3.1 collective-permute-start.4
  1625.6 2.9 collective-permute-done.5
  1628.6 1.4 convolution_select_fusion
  1632.4 2.9 fusion.14
  1635.3 3.3 reshape.865
  1638.7 192.7 %all-reduce.14.cloned.1.call-done = f32[1024,3,256]{2,1,0:T(4,128)} async-done(((f32[1024,3,256]{2,1,0:T(4,128)}), f32[1024,3,256]{2,1,0:T(4,128)}) %all-reduce.14.cloned.1.call-update) | async-done | bytes 3145744
  1832.3 13.5 psum.54
  1846.5 130.2 %psum.55 = f32[]{:T(128)} all-reduce(f32[]{:T(128)} %multiply_reduce_fusion), channel_id=1, replica_groups=mesh['det'=64,'tm'=4] {'det'}, use_global_device_ids=true, to_apply=%region_78.79 | all-reduce | flops 1 | bytes 8 | tf_op jit(solution)/shard_map/psum | solution.py:83
  (244 shorter events, 83.5 us)
Async XLA Ops:
  7.2 886.2 %reduce-scatter.2.cloned.1.call-start = ((), (), s32[]{:S(2)}) async-start(), calls=%async_computation.1 | async-start | bytes 9584640 | tf_op jit(solution)/shard_map/reduce_scatter | solution.py:136
  8.6 691.0 %collective-permute-start = (f32[1,64]{1,0:T(1,128)S(1)}, f32[1,64]{1,0:T(1,128)S(1)}, u32[]{:S(2)}, u32[]{:S(2)}) collective-permute-start(f32[1,64]{1,0:T(1,128)S(1)} %get-tuple-element.57), channel_id=1, source_target_pairs={{0,1},{1,2},{2,3},{4,5},{5,6},{6,7},{8,9},{9,10},{10,11},{12,13},{... | collective-permute-start | bytes 776 | tf_op jit(solution)/shard_map/ppermute | solution.py:25
  12.6 687.0 %collective-permute-start.1 = (f32[1,64]{1,0:T(1,128)S(1)}, f32[1,64]{1,0:T(1,128)S(1)}, u32[]{:S(2)}, u32[]{:S(2)}) collective-permute-start(f32[1,64]{1,0:T(1,128)S(1)} %get-tuple-element.56), channel_id=1, source_target_pairs={{1,0},{2,1},{3,2},{5,4},{6,5},{7,6},{9,8},{10,9},{11,10},{13,12},{... | collective-permute-start | bytes 776 | tf_op jit(solution)/shard_map/ppermute | solution.py:27
  107.8 592.1 %copy-start.44 = (s32[384]{0:T(512)}, s32[384]{0:T(512)S(1)}, u32[]{:S(2)}) copy-start(s32[384]{0:T(512)S(1)} %iota_add_fusion) | copy-start | bytes 4612
  107.8 593.2 %copy-start.41 = (s32[64,2]{0,1:T(2,128)}, s32[64,2]{0,1:T(2,128)S(1)}, u32[]{:S(2)}) copy-start(s32[64,2]{0,1:T(2,128)S(1)} %multiply_add_fusion.3) | copy-start | bytes 1540
  113.3 584.0 %copy-start.37 = (f32[1,1,1024]{2,1,0:T(1,128)S(1)}, f32[1,1,1024]{2,1,0:T(1,128)}, u32[]{:S(2)}) copy-start(f32[1,1,1024]{2,1,0:T(1,128)} %param.11) | copy-start | bytes 12292
  113.3 584.7 %copy-start.47 = (s32[1,128]{1,0:T(1,128)S(1)}, s32[1,128]{1,0:T(1,128)}, u32[]{:S(2)}) copy-start(s32[1,128]{1,0:T(1,128)} %param.14) | copy-start | bytes 1540
  113.3 585.6 %copy-start.45 = (s32[1,1,1024]{2,1,0:T(1,128)S(1)}, s32[1,1,1024]{2,1,0:T(1,128)}, u32[]{:S(2)}) copy-start(s32[1,1,1024]{2,1,0:T(1,128)} %param.12) | copy-start | bytes 12292
  113.3 587.6 %copy-start.38 = (s32[1,1,4]{2,1,0:T(1,128)S(1)}, s32[1,1,4]{2,1,0:T(1,128)}, u32[]{:S(2)}) copy-start(s32[1,1,4]{2,1,0:T(1,128)} %param.13) | copy-start | bytes 52
  697.3 12.4 copy-start.19
  697.5 3.0 copy-start.35
  697.5 12.2 copy-start.36
  698.9 10.8 copy-start.1
  699.6 0.9 copy-start.46
  737.3 205.5 %all-reduce.10.cloned.1.call-start = ((), (), s32[]{:S(2)}) async-start(), calls=%async_computation.2 | async-start | bytes 294912 | tf_op jit(solution)/shard_map/psum | solution.py:137
  893.3 135.6 %all-gather.3.cloned.1.call-start = ((), (), s32[]{:S(2)}) async-start(), calls=%async_computation.3 | async-start | bytes 3194880 | tf_op jit(solution)/shard_map/all_gather | solution.py:165
  944.2 1.5 copy-start.20
  944.2 1.5 copy-start.16
  944.2 2.9 copy-start.23
  945.7 1.4 copy-start.26
  945.7 1.4 copy-start.4
  947.1 0.6 copy-start.7
  948.4 307.7 %all-reduce.12.cloned.1.call-start = ((), (), s32[]{:S(2)}) async-start(), calls=%async_computation.5 | async-start | bytes 8388608
  1041.8 14.6 copy-start.39
  1041.8 14.6 copy-start.42
  1045.4 4.4 collective-permute-start.2
  1048.5 4.3 collective-permute-start.3
  1063.0 0.7 copy-start.48
  1063.0 207.5 %copy-start = (f32[16,9,256]{2,0,1:T(8,128)S(1)}, f32[16,9,256]{2,0,1:T(8,128)}, u32[]{:S(2)}) copy-start(f32[16,9,256]{2,0,1:T(8,128)} %all-reduce.10.cloned.1.call-done) | copy-start | bytes 442372
  1063.0 207.6 %copy-start.5 = (f32[16,1,256]{2,0,1:T(8,128)S(1)}, f32[16,1,256]{2,0,1:T(8,128)}, u32[]{:S(2)}) copy-start(f32[16,1,256]{2,0,1:T(8,128)} %copy-done.4) | copy-start | bytes 49156
  1063.0 207.6 %copy-start.8 = (f32[16,1,256]{2,0,1:T(8,128)S(1)}, f32[16,1,256]{2,0,1:T(8,128)}, u32[]{:S(2)}) copy-start(f32[16,1,256]{2,0,1:T(8,128)} %copy-done.7) | copy-start | bytes 49156
  1063.0 339.8 %copy-start.17 = (f32[16,1,256]{2,0,1:T(8,128)S(1)}, f32[16,1,256]{2,0,1:T(8,128)}, u32[]{:S(2)}) copy-start(f32[16,1,256]{2,0,1:T(8,128)} %copy-done.16) | copy-start | bytes 49156
  1063.0 339.8 %copy-start.21 = (f32[16,1,256]{2,0,1:T(8,128)S(1)}, f32[16,1,256]{2,0,1:T(8,128)}, u32[]{:S(2)}) copy-start(f32[16,1,256]{2,0,1:T(8,128)} %copy-done.20) | copy-start | bytes 49156
  1063.0 339.8 %copy-start.24 = (f32[16,1,256]{2,0,1:T(8,128)S(1)}, f32[16,1,256]{2,0,1:T(8,128)}, u32[]{:S(2)}) copy-start(f32[16,1,256]{2,0,1:T(8,128)} %copy-done.23) | copy-start | bytes 49156
  1063.0 339.8 %copy-start.27 = (f32[16,1,256]{2,0,1:T(8,128)S(1)}, f32[16,1,256]{2,0,1:T(8,128)}, u32[]{:S(2)}) copy-start(f32[16,1,256]{2,0,1:T(8,128)} %copy-done.26) | copy-start | bytes 49156
  1063.0 339.8 %copy-start.29 = (f32[16,1,256]{2,0,1:T(8,128)S(1)}, f32[16,1,256]{2,0,1:T(8,128)}, u32[]{:S(2)}) copy-start(f32[16,1,256]{2,0,1:T(8,128)} %get-tuple-element.26) | copy-start | bytes 49156
  1063.0 339.8 %copy-start.31 = (f32[16,1,256]{2,0,1:T(8,128)S(1)}, f32[16,1,256]{2,0,1:T(8,128)}, u32[]{:S(2)}) copy-start(f32[16,1,256]{2,0,1:T(8,128)} %get-tuple-element.30) | copy-start | bytes 49156
  1063.0 339.8 %copy-start.33 = (f32[16,1,256]{2,0,1:T(8,128)S(1)}, f32[16,1,256]{2,0,1:T(8,128)}, u32[]{:S(2)}) copy-start(f32[16,1,256]{2,0,1:T(8,128)} %get-tuple-element.33) | copy-start | bytes 49156
  1063.1 541.4 %all-gather.5.cloned.1.call-start = ((), (), s32[]{:S(2)}) async-start(), calls=%async_computation.4 | async-start | bytes 3194880 | tf_op jit(solution)/shard_map/all_gather | solution.py:165
  1402.7 0.6 copy-start.2
  1402.8 201.7 %copy-start.10 = (f32[16,1,256]{2,0,1:T(8,128)}, f32[16,1,256]{2,0,1:T(8,128)S(1)}, u32[]{:S(2)}) copy-start(f32[16,1,256]{2,0,1:T(8,128)S(1)} %get-tuple-element.37) | copy-start | bytes 49156
  1402.8 201.7 %copy-start.12 = (f32[16,1,256]{2,0,1:T(8,128)}, f32[16,1,256]{2,0,1:T(8,128)S(1)}, u32[]{:S(2)}) copy-start(f32[16,1,256]{2,0,1:T(8,128)S(1)} %get-tuple-element.38) | copy-start | bytes 49156
  1402.8 201.7 %copy-start.14 = (f32[16,1,256]{2,0,1:T(8,128)}, f32[16,1,256]{2,0,1:T(8,128)S(1)}, u32[]{:S(2)}) copy-start(f32[16,1,256]{2,0,1:T(8,128)S(1)} %get-tuple-element.39) | copy-start | bytes 49156
  1530.5 300.9 %all-reduce.14.cloned.1.call-start = ((), (), s32[]{:S(2)}) async-start(), calls=%async_computation.6 | async-start | bytes 8388608
  1617.4 14.6 copy-start.40
  1617.4 14.6 copy-start.43
  1621.0 4.4 collective-permute-start.4
  1624.1 4.3 collective-permute-start.5
  1638.6 207.3 %copy-start.6 = (f32[16,1,256]{2,0,1:T(8,128)S(1)}, f32[16,1,256]{2,0,1:T(8,128)}, u32[]{:S(2)}) copy-start(f32[16,1,256]{2,0,1:T(8,128)} %copy-done.4) | copy-start | bytes 49156
  1638.6 207.3 %copy-start.9 = (f32[16,1,256]{2,0,1:T(8,128)S(1)}, f32[16,1,256]{2,0,1:T(8,128)}, u32[]{:S(2)}) copy-start(f32[16,1,256]{2,0,1:T(8,128)} %copy-done.7) | copy-start | bytes 49156
  1638.6 207.3 %copy-start.11 = (f32[16,1,256]{2,0,1:T(8,128)S(1)}, f32[16,1,256]{2,0,1:T(8,128)}, u32[]{:S(2)}) copy-start(f32[16,1,256]{2,0,1:T(8,128)} %copy-done.10) | copy-start | bytes 49156
  1638.6 207.3 %copy-start.13 = (f32[16,1,256]{2,0,1:T(8,128)S(1)}, f32[16,1,256]{2,0,1:T(8,128)}, u32[]{:S(2)}) copy-start(f32[16,1,256]{2,0,1:T(8,128)} %copy-done.12) | copy-start | bytes 49156
  1638.6 207.3 %copy-start.15 = (f32[16,1,256]{2,0,1:T(8,128)S(1)}, f32[16,1,256]{2,0,1:T(8,128)}, u32[]{:S(2)}) copy-start(f32[16,1,256]{2,0,1:T(8,128)} %copy-done.14) | copy-start | bytes 49156
  1638.6 339.4 %copy-start.3 = (f32[16,3,256]{2,0,1:T(8,128)S(1)}, f32[16,3,256]{2,0,1:T(8,128)}, u32[]{:S(2)}) copy-start(f32[16,3,256]{2,0,1:T(8,128)} %copy-done.2) | copy-start | bytes 147460
  1638.6 340.1 %copy-start.18 = (f32[16,1,256]{2,0,1:T(8,128)S(1)}, f32[16,1,256]{2,0,1:T(8,128)}, u32[]{:S(2)}) copy-start(f32[16,1,256]{2,0,1:T(8,128)} %copy-done.16) | copy-start | bytes 49156
  1638.6 340.1 %copy-start.22 = (f32[16,1,256]{2,0,1:T(8,128)S(1)}, f32[16,1,256]{2,0,1:T(8,128)}, u32[]{:S(2)}) copy-start(f32[16,1,256]{2,0,1:T(8,128)} %copy-done.20) | copy-start | bytes 49156
  1638.6 340.1 %copy-start.25 = (f32[16,1,256]{2,0,1:T(8,128)S(1)}, f32[16,1,256]{2,0,1:T(8,128)}, u32[]{:S(2)}) copy-start(f32[16,1,256]{2,0,1:T(8,128)} %copy-done.23) | copy-start | bytes 49156
  1638.6 340.0 %copy-start.28 = (f32[16,1,256]{2,0,1:T(8,128)S(1)}, f32[16,1,256]{2,0,1:T(8,128)}, u32[]{:S(2)}) copy-start(f32[16,1,256]{2,0,1:T(8,128)} %copy-done.26) | copy-start | bytes 49156
  1638.6 340.0 %copy-start.30 = (f32[16,1,256]{2,0,1:T(8,128)S(1)}, f32[16,1,256]{2,0,1:T(8,128)}, u32[]{:S(2)}) copy-start(f32[16,1,256]{2,0,1:T(8,128)} %get-tuple-element.26) | copy-start | bytes 49156
  1638.7 340.0 %copy-start.32 = (f32[16,1,256]{2,0,1:T(8,128)S(1)}, f32[16,1,256]{2,0,1:T(8,128)}, u32[]{:S(2)}) copy-start(f32[16,1,256]{2,0,1:T(8,128)} %get-tuple-element.30) | copy-start | bytes 49156
  1638.7 340.0 %copy-start.34 = (f32[16,1,256]{2,0,1:T(8,128)S(1)}, f32[16,1,256]{2,0,1:T(8,128)}, u32[]{:S(2)}) copy-start(f32[16,1,256]{2,0,1:T(8,128)} %get-tuple-element.33) | copy-start | bytes 49156
Sparse Core Ops, SparseCore 0:
  737.4 155.8 reduce-scatter.1
  895.6 47.0 all-reduce.9
  948.5 80.3 all-gather.2
  1063.2 192.8 all-reduce.11
  1530.7 73.7 all-gather.4
  1638.8 192.5 all-reduce.13
where the time goes:
time: 1990 us
  waiting for transfers between devices  749 us (38%)
  local copies, waits for them, and re-layouts  649 us (33%)
  blocking collectives  412 us (21%)
  other arithmetic  107 us (5%)
  matrix products  30 us (2%)
  between operations  24.3 us (1%)
    gather x2, local copies, waits for them, and re-layouts, toeplitz_matrix(): return jnp.where(inside[None], lags[:, clipped], 0.0)  584 us
    psum x3, blocking collectives, global_dot(): return lax.psum(jnp.sum(left * right), 'det')  385 us
    unnamed x8, waiting for transfers between devices  384 us
    reduce_scatter x1, waiting for transfers between devices, to_owner_blocks(): lax.psum_scatter(whole_map, 'det', scatter_dimension=0, tiled=True)  156 us
    all_gather x2, waiting for transfers between devices, per_device(): from_whole_map = lax.all_gather(direction, 'det', axis=0, tiled=True)  154 us
    reduce_sum x64, other arithmetic, lag_table(): jnp.sum(filter_taps[..., :BAND + 1 - shift_lag] * filter_taps[..., shift_...  91.9 us
    psum x1, waiting for transfers between devices, to_owner_blocks(): owned_map = lax.psum(owned_map, 'tm')  49.2 us
  transfers between devices with their start and end apart: 12, of which 8 were waited for; matrix products, arithmetic and copies ran while one was open for 34% of the time, Pallas kernels for 0%

commit v1 on v0

--- a/solution.py
+++ b/solution.py
@@ -162,7 +162,8 @@
     direction = descent
     product_now = global_dot(residual, descent)
     for iteration in range(ITERS):
-        from_whole_map = lax.all_gather(direction, "det", axis=0, tiled=True)
+        sent = jnp.stack([direction] * lax.axis_size("det"))
+        from_whole_map = jnp.concatenate(lax.all_to_all(sent, "det", 0, 0), axis=0)
         from_grouped = from_whole_map.reshape(det_count, BPD, 3 * BLK)
         picked = jnp.einsum("ocb,obx->ocx", place_pick, from_grouped, precision=highest)
         fetched = picked.reshape(hit_total, 3, BLK)

time: 1990 us -> 1960 us (0.985)
  blocking collectives: 412 us -> 577 us
  waiting for transfers between devices: 749 us -> 593 us
  local copies, waits for them, and re-layouts: 649 us -> 627 us
    all_to_all x0 -> x2, blocking collectives: none -> 165 us  [per_device(): from_whole_map = jnp.concatenate(lax.all_to_all(sent, 'det', 0, 0), axis=0)]
    all_gather x2 -> x0, waiting for transfers between devices: 154 us -> none  [per_device(): from_whole_map = lax.all_gather(direction, 'det', axis=0, tiled=True)]
    unnamed x8 -> x6, waiting for transfers between devices: 384 us -> 382 us
  transfers between devices with their start and end apart: 12 -> 10, of which waited for: 8 -> 6; matrix products, arithmetic and copies ran while one was open for 34% -> 35% of each run, Pallas kernels for 0% -> 0%
where the time goes in v1:
time: 1960 us; the launch traced here: 1950 us
  local copies, waits for them, and re-layouts  627 us (32%)
  waiting for transfers between devices  593 us (30%)
  blocking collectives  577 us (29%)
  other arithmetic  101 us (5%)
  between operations  23.6 us (1%)
  matrix products  21 us (1%)
    gather x2, local copies, waits for them, and re-layouts, toeplitz_matrix(): return jnp.where(inside[None], lags[:, clipped], 0.0)  584 us
    psum x3, blocking collectives, global_dot(): return lax.psum(jnp.sum(left * right), 'det')  385 us
    unnamed x6, waiting for transfers between devices  382 us
    all_to_all x2, blocking collectives, per_device(): from_whole_map = jnp.concatenate(lax.all_to_all(sent, 'det', 0, 0), axis=0)  165 us
    reduce_scatter x1, waiting for transfers between devices, to_owner_blocks(): lax.psum_scatter(whole_map, 'det', scatter_dimension=0, tiled=True)  156 us
    reduce_sum x64, other arithmetic, lag_table(): jnp.sum(filter_taps[..., :BAND + 1 - shift_lag] * filter_taps[..., shift_...  91.9 us
    psum x1, waiting for transfers between devices, to_owner_blocks(): owned_map = lax.psum(owned_map, 'tm')  49.2 us
  transfers between devices with their start and end apart: 10, of which 6 were waited for; matrix products, arithmetic and copies ran while one was open for 35% of the time, Pallas kernels for 0%

profile of v1, /device:TPU:1, one launch (start us, length us, event | category | flops | bytes accessed | tf_op | source)
XLA Modules:
  0.0 1955.0 jit_solution(3117108766312398189)
XLA Ops:
  8.6 3.9 collective-permute-start
  15.2 1.5 multiply_reduce_fusion.62
  16.7 1.4 multiply_reduce_fusion.61
  20.9 1.5 multiply_reduce_fusion.58
  23.8 1.5 multiply_reduce_fusion.56
  25.3 1.5 multiply_reduce_fusion.55
  26.7 1.4 multiply_reduce_fusion.54
  28.1 1.5 multiply_reduce_fusion.53
  29.6 1.4 multiply_reduce_fusion.52
  32.5 1.4 multiply_reduce_fusion.50
  33.9 1.5 multiply_reduce_fusion.49
  35.4 1.4 multiply_reduce_fusion.48
  38.2 1.5 multiply_reduce_fusion.46
  39.6 1.5 multiply_reduce_fusion.45
  44.0 1.4 multiply_reduce_fusion.42
  45.4 1.5 multiply_reduce_fusion.41
  48.3 1.5 multiply_reduce_fusion.39
  51.2 1.5 multiply_reduce_fusion.37
  52.6 1.5 multiply_reduce_fusion.36
  54.1 1.4 multiply_reduce_fusion.35
  55.6 1.4 multiply_reduce_fusion.34
  57.0 1.5 multiply_reduce_fusion.33
  59.9 1.5 multiply_reduce_fusion.31
  61.4 1.4 multiply_reduce_fusion.30
  64.2 1.5 multiply_reduce_fusion.28
  65.7 1.5 multiply_reduce_fusion.27
  69.9 1.5 multiply_reduce_fusion.24
  71.4 1.4 multiply_reduce_fusion.23
  74.3 1.4 multiply_reduce_fusion.21
  77.1 1.5 multiply_reduce_fusion.19
  80.0 1.5 multiply_reduce_fusion.17
  82.8 1.4 multiply_reduce_fusion.15
  84.2 1.5 multiply_reduce_fusion.14
  88.5 1.5 multiply_reduce_fusion.12
  91.4 1.5 multiply_reduce_fusion.10
  92.9 1.4 multiply_reduce_fusion.9
  94.3 1.5 multiply_reduce_fusion.8
  95.8 1.5 multiply_reduce_fusion.7
  97.2 1.4 multiply_reduce_fusion.6
  98.7 1.5 multiply_reduce_fusion.5
  101.5 1.5 multiply_reduce_fusion.65
  104.4 1.4 multiply_reduce_fusion.63
  113.4 583.8 %gather_fusion = f32[98304]{0:T(1024)S(1)} fusion(f32[65]{0:T(128)S(1)} %bitcast_dynamic-update-slice_fusion, s32[98304]{0:T(1024)S(1)} %broadcast_clamp_fusion), kind=kCustom, calls=%fused_computation | custom fusion | bytes 1179648 | tf_op jit(solution)/shard_map/gather | solution.py:52
  701.7 7.9 fusion
  709.6 12.7 reshape.866
  722.3 14.9 copy.43
  737.2 155.9 %reduce-scatter.2.cloned.1.call-done = f32[16,9,256]{2,0,1:T(8,128)} async-done(((f32[1024,9,256]{2,0,1:T(8,128)}), f32[16,9,256]{2,0,1:T(8,128)}) %reduce-scatter.2.cloned.1.call-update) | async-done | bytes 147472 | tf_op jit(solution)/shard_map/reduce_scatter | solution.py:136
  893.3 49.2 %all-reduce.10.cloned.1.call-done = f32[16,9,256]{2,0,1:T(8,128)} async-done(((f32[16,9,256]{2,0,1:T(8,128)}), f32[16,9,256]{2,0,1:T(8,128)}) %all-reduce.10.cloned.1.call-update) | async-done | bytes 147472 | tf_op jit(solution)/shard_map/psum | solution.py:137
  945.5 85.7 %all_to_all.10 = f32[64,16,3,256]{3,1,2,0:T(8,128)S(1)} all-to-all(f32[64,16,3,256]{3,1,2,0:T(8,128)S(1)} %stack.460), channel_id=1, replica_groups=mesh['det'=64,'tm'=4] {'det'}, dimensions={0} | all-to-all | bytes 6291456 | tf_op jit(solution)/shard_map/all_to_all | solution.py:166
  1034.3 2.1 collective-permute-start.2
  1037.8 2.9 collective-permute-done.3
  1042.2 2.1 fusion.16
  1044.4 3.3 reshape.872
  1049.6 190.7 %all-reduce.12.cloned.1.call-done = f32[1024,3,256]{2,1,0:T(4,128)} async-done(((f32[1024,3,256]{2,1,0:T(4,128)}), f32[1024,3,256]{2,1,0:T(4,128)}) %all-reduce.12.cloned.1.call-update) | async-done | bytes 3145744
  1241.2 13.5 psum.51
  1255.4 130.2 %all-reduce.5 = (f32[]{:T(128)}, f32[]{:T(128)}) all-reduce(f32[]{:T(128)} %get-tuple-element.19, f32[]{:T(128)} %get-tuple-element.18), channel_id=1, replica_groups=mesh['det'=64,'tm'=4] {'det'}, use_global_device_ids=true, to_apply=%region_68.69 | all-reduce | flops 2 | bytes 16 | tf_op jit(solution)/shard_map/psum | solution.py:83
  1387.6 124.7 %psum.53 = f32[]{:T(128)} all-reduce(f32[]{:T(128)} %multiply_reduce_fusion.1), channel_id=1, replica_groups=mesh['det'=64,'tm'=4] {'det'}, use_global_device_ids=true, to_apply=%region_74.75 | all-reduce | flops 1 | bytes 8 | tf_op jit(solution)/shard_map/psum | solution.py:83
  1514.0 79.3 %all_to_all.11 = f32[64,16,3,256]{3,1,2,0:T(8,128)S(1)} all-to-all(f32[64,16,3,256]{3,1,2,0:T(8,128)S(1)} %stack.466), channel_id=1, replica_groups=mesh['det'=64,'tm'=4] {'det'}, dimensions={0} | all-to-all | bytes 6291456 | tf_op jit(solution)/shard_map/all_to_all | solution.py:166
  1599.2 2.9 collective-permute-done.5
  1603.7 2.1 fusion.14
  1605.8 3.3 reshape.878
  1609.1 191.5 %all-reduce.14.cloned.1.call-done = f32[1024,3,256]{2,1,0:T(4,128)} async-done(((f32[1024,3,256]{2,1,0:T(4,128)}), f32[1024,3,256]{2,1,0:T(4,128)}) %all-reduce.14.cloned.1.call-update) | async-done | bytes 3145744
  1801.5 13.5 psum.54
  1815.7 130.2 %psum.55 = f32[]{:T(128)} all-reduce(f32[]{:T(128)} %multiply_reduce_fusion), channel_id=1, replica_groups=mesh['det'=64,'tm'=4] {'det'}, use_global_device_ids=true, to_apply=%region_78.79 | all-reduce | flops 1 | bytes 8 | tf_op jit(solution)/shard_map/psum | solution.py:83
  (158 shorter events, 65.3 us)
Async XLA Ops:
  7.2 885.9 %reduce-scatter.2.cloned.1.call-start = ((), (), s32[]{:S(2)}) async-start(), calls=%async_computation.3 | async-start | bytes 9584640 | tf_op jit(solution)/shard_map/reduce_scatter | solution.py:136
  8.6 690.9 %collective-permute-start = (f32[1,64]{1,0:T(1,128)S(1)}, f32[1,64]{1,0:T(1,128)S(1)}, u32[]{:S(2)}, u32[]{:S(2)}) collective-permute-start(f32[1,64]{1,0:T(1,128)S(1)} %get-tuple-element.57), channel_id=1, source_target_pairs={{0,1},{1,2},{2,3},{4,5},{5,6},{6,7},{8,9},{9,10},{10,11},{12,13},{... | collective-permute-start | bytes 776 | tf_op jit(solution)/shard_map/ppermute | solution.py:25
  12.6 687.0 %collective-permute-start.1 = (f32[1,64]{1,0:T(1,128)S(1)}, f32[1,64]{1,0:T(1,128)S(1)}, u32[]{:S(2)}, u32[]{:S(2)}) collective-permute-start(f32[1,64]{1,0:T(1,128)S(1)} %get-tuple-element.56), channel_id=1, source_target_pairs={{1,0},{2,1},{3,2},{5,4},{6,5},{7,6},{9,8},{10,9},{11,10},{13,12},{... | collective-permute-start | bytes 776 | tf_op jit(solution)/shard_map/ppermute | solution.py:27
  113.3 584.0 %copy-start.3 = (f32[1,1,1024]{2,1,0:T(1,128)S(1)}, f32[1,1,1024]{2,1,0:T(1,128)}, u32[]{:S(2)}) copy-start(f32[1,1,1024]{2,1,0:T(1,128)} %param.11) | copy-start | bytes 12292
  113.3 584.7 %copy-start.6 = (s32[1,128]{1,0:T(1,128)S(1)}, s32[1,128]{1,0:T(1,128)}, u32[]{:S(2)}) copy-start(s32[1,128]{1,0:T(1,128)} %param.14) | copy-start | bytes 1540
  113.3 585.5 %copy-start.5 = (s32[1,1,1024]{2,1,0:T(1,128)S(1)}, s32[1,1,1024]{2,1,0:T(1,128)}, u32[]{:S(2)}) copy-start(s32[1,1,1024]{2,1,0:T(1,128)} %param.12) | copy-start | bytes 12292
  113.3 587.6 %copy-start.4 = (s32[1,1,4]{2,1,0:T(1,128)S(1)}, s32[1,1,4]{2,1,0:T(1,128)}, u32[]{:S(2)}) copy-start(s32[1,1,4]{2,1,0:T(1,128)} %param.13) | copy-start | bytes 52
  697.3 343.5 %copy-start.1 = (f32[1,384,256]{2,1,0:T(8,128)}, f32[1,384,256]{2,1,0:T(8,128)S(1)}, u32[]{:S(2)}) copy-start(f32[1,384,256]{2,1,0:T(8,128)S(1)} %reshape.880) | copy-start | bytes 1179652
  737.2 205.4 %all-reduce.10.cloned.1.call-start = ((), (), s32[]{:S(2)}) async-start(), calls=%async_computation.4 | async-start | bytes 294912 | tf_op jit(solution)/shard_map/psum | solution.py:137
  893.1 347.2 %all-reduce.12.cloned.1.call-start = ((), (), s32[]{:S(2)}) async-start(), calls=%async_computation.5 | async-start | bytes 8388608
  1034.3 3.4 collective-permute-start.2
  1036.3 4.3 collective-permute-start.3
  1047.6 0.7 copy-start.7
  1047.7 207.1 %copy-start = (f32[16,9,256]{2,0,1:T(8,128)S(1)}, f32[16,9,256]{2,0,1:T(8,128)}, u32[]{:S(2)}) copy-start(f32[16,9,256]{2,0,1:T(8,128)} %all-reduce.10.cloned.1.call-done) | copy-start | bytes 442372
  1047.7 752.9 %all-reduce.14.cloned.1.call-start = ((), (), s32[]{:S(2)}) async-start(), calls=%async_computation.6 | async-start | bytes 8388608
  1593.6 8.7 copy-start.2
  1596.5 2.6 collective-permute-start.4
  1597.8 4.3 collective-permute-start.5
Sparse Core Ops, SparseCore 0:
  737.3 155.7 reduce-scatter.1
  895.4 47.0 all-reduce.9
  1047.8 192.4 all-reduce.11
  1609.2 191.3 all-reduce.13
